TPU v7x, 128 devices: a whole 4x4x4 slice. The times are simulated.
128 devices in a mesh: gx: 16 (over z_lo, y, core), gy: 8 (over x, z_hi).
Axes of the slice: x: 4, y: 4, z: 4 (z_hi: 2, z_lo: 2; z = z_hi * 2 + z_lo), core: 2. Of those that a mesh axis runs over, the one named last changes fastest.
Arguments:
- field_e: float32 [3, 256, 128, 256], P(None, 'gx', 'gy'), may hold values from -6 to 6
- field_h: float32 [3, 256, 128, 256], P(None, 'gx', 'gy'), may hold values from -6 to 6
- density: float32 [2, 8, 8, 2097152], P(None, None, None, ('gx', 'gy')), may hold values from -1.8 to 1.8
- dipole: float32 [3, 2097152], P(None, ('gx', 'gy')), may hold values from -6 to 6
- levels: float32 [8], replicated, may hold values from -3 to 3
- coupling: float32 [8, 8], replicated, may hold values from -2 to 2
- rates: float32 [8, 8], replicated, may hold values from 0.1 to 3
- tile_cells: int32 [16384], P(('gx', 'gy')), may hold values from 0 to 511, as said below
- tile_owner: int32 [16384, 1], P(('gx', 'gy')), may hold values from 0 to 127; in each aligned block of 128 rows (0 to 127, 128 to 255, ...) at most 2 rows name the same one
- emitter_offsets: int32 [16384, 64], P(('gx', 'gy')), may hold values from 0 to 127
Outputs:
- electric_out: float32 [3, 256, 128, 256], P(None, 'gx', 'gy')
- magnetic_out: float32 [3, 256, 128, 256], P(None, 'gx', 'gy')
- density_out: float32 [2, 8, 8, 2097152], P(None, None, None, ('gx', 'gy'))
Inputs may be any that keep to these rules, and one draw needn't show every extreme that they name: `tile_cells`: within one device's 128 entries the local tile numbers are distinct. `tile_owner`: among the 128 tiles of one device no owner is named more than 2 times.
All inputs are finite; a program needn't handle non-finite values.
Results may differ from a plain program's by a relative error of at most 0.0003.
Values sent between devices are 32-bit elements; how exact they have to be, the bound alone decides.
A program may use at most 320 MiB of HBM per device.

v0:
```python
import jax
import jax.numpy as jnp
from jax import lax
from jax.sharding import PartitionSpec as P

TILE = 128
STEPS = 4


courant = 0.5
time_step = 0.12


def passed_along(block, axis, distance):
    devices = range(lax.axis_size(axis))
    route = [(i - distance, i) for i in devices if i - distance in devices]
    return lax.ppermute(block, axis, route)


def forward(values_in, beyond, along):
    length = values_in.shape[along]
    return (
        jnp.concatenate([lax.slice_in_dim(values_in, 1, length, axis=along), beyond], axis=along)
        - values_in
    )


def backward(values_in, behind_slab, along):
    length = values_in.shape[along]
    return values_in - jnp.concatenate(
        [behind_slab, lax.slice_in_dim(values_in, 0, length - 1, axis=along)], axis=along
    )


def zero_edge(values_in, along):
    return jnp.zeros_like(lax.slice_in_dim(values_in, 0, 1, axis=along))


def curl_ahead(fields, planes, rows):
    curl_one = forward(fields[2], rows[1], 1) - forward(fields[1], zero_edge(fields[1], 2), 2)
    curl_two = forward(fields[0], zero_edge(fields[0], 2), 2) - forward(fields[2], planes[1], 0)
    curl_three = forward(fields[1], planes[0], 0) - forward(fields[0], rows[0], 1)
    return jnp.stack([curl_one, curl_two, curl_three])


def curl_behind(fields, planes, rows):
    curl_one = backward(fields[2], rows[1], 1) - backward(fields[1], zero_edge(fields[1], 2), 2)
    curl_two = backward(fields[0], zero_edge(fields[0], 2), 2) - backward(fields[2], planes[1], 0)
    curl_three = backward(fields[1], planes[0], 0) - backward(fields[0], rows[0], 1)
    return jnp.stack([curl_one, curl_two, curl_three])


def commutator(symmetric, matrix):
    result = jnp.zeros_like(matrix)
    for inner in range(matrix.shape[0]):
        result = result + symmetric[:, inner][:, None, None] * matrix[inner][None, :, :]
        result = result - matrix[:, inner][:, None, :] * symmetric[inner][None, :, None]
    return result


def advance_driven(states, driving, levels, symmetric, damping):
    real_part = states[0]
    imag_part = states[1]
    spacing = (levels[:, None] - levels[None, :])[:, :, None]
    decays = damping[:, :, None]
    comm_imag = commutator(symmetric, imag_part)
    comm_real = commutator(symmetric, real_part)
    change_real = spacing * imag_part + driving * comm_imag - decays * real_part
    change_imag = -spacing * real_part - driving * comm_real - decays * imag_part
    moved = time_step * jnp.sum(symmetric[:, :, None] * change_real, axis=(0, 1))
    updated = jnp.stack([real_part + time_step * change_real, imag_part + time_step * change_imag])
    return (updated, moved)


def advance(states, orient, samples, levels, symmetric, damping):
    driving = orient[0] * samples[0] + orient[1] * samples[1] + orient[2] * samples[2]
    updated, moved = advance_driven(states, driving, levels, symmetric, damping)
    return (updated, moved[None, :] * orient)


def body(
    field_e,
    field_h,
    density,
    dipole,
    levels,
    coupling,
    rates,
    tile_cells,
    tile_owner,
    emitter_offsets,
):
    count_x = lax.axis_size("gx")
    count_y = lax.axis_size("gy")
    devices = count_x * count_y
    tile_count = tile_cells.shape[0]
    per_tile = emitter_offsets.shape[1]
    capacity = density.shape[3] // (devices * per_tile)
    symmetric = 0.5 * (coupling + coupling.T)
    damping = 0.5 * (rates + rates.T) * (1.0 - jnp.eye(coupling.shape[0], dtype=jnp.float32))
    positions = (tile_cells[:, None] * TILE + emitter_offsets).reshape(-1)
    owners = tile_owner[:, 0]
    ordinal = jnp.arange(tile_count, dtype=jnp.int32)
    earlier = ordinal[None, :] < ordinal[:, None]
    matches = owners[:, None] == owners[None, :]
    ranking = jnp.sum(jnp.where(matches & earlier, 1, 0), axis=1).astype(jnp.int32)
    slot_rows = owners * capacity + ranking
    for repeat in range(STEPS):
        ahead_planes = passed_along(field_e[1:3, 0:1], "gx", -1)
        ahead_rows = passed_along(field_e[0::2, :, 0:1], "gy", -1)
        field_h = field_h - courant * curl_ahead(field_e, ahead_planes, ahead_rows)
        behind_planes = passed_along(field_h[1:3, -1:], "gx", 1)
        behind_rows = passed_along(field_h[0::2, :, -1:], "gy", 1)
        field_e = field_e + courant * curl_behind(field_h, behind_planes, behind_rows)
        flattened = field_e.reshape(3, -1)
        samples = flattened[:, positions].reshape(3, tile_count, per_tile)
        outgoing = (
            jnp.zeros((3, devices * capacity, per_tile), jnp.float32)
            .at[:, slot_rows, :]
            .set(samples)
        )
        incoming = lax.all_to_all(
            outgoing.reshape(3, devices, -1), ("gx", "gy"), split_axis=1, concat_axis=1, tiled=True
        )
        density, feed_terms = advance(
            density, dipole, incoming.reshape(3, -1), levels, symmetric, damping
        )
        returned = lax.all_to_all(
            feed_terms.reshape(3, devices, -1),
            ("gx", "gy"),
            split_axis=1,
            concat_axis=1,
            tiled=True,
        )
        back_terms = returned.reshape(3, devices * capacity, per_tile)[:, slot_rows, :].reshape(
            3, -1
        )
        flattened = flattened.at[:, positions].add(-back_terms)
        field_e = flattened.reshape(field_e.shape)
    return (field_e, field_h, density)


def solution(mesh):
    placed = (
        P(None, "gx", "gy", None),
        P(None, "gx", "gy", None),
        P(None, None, None, ("gx", "gy")),
        P(None, ("gx", "gy")),
        P(),
        P(),
        P(),
        P(("gx", "gy")),
        P(("gx", "gy"), None),
        P(("gx", "gy"), None),
    )
    return jax.shard_map(
        body,
        mesh=mesh,
        in_specs=placed,
        out_specs=(
            P(None, "gx", "gy", None),
            P(None, "gx", "gy", None),
            P(None, None, None, ("gx", "gy")),
        ),
        check_vma=False,
    )
```

profile of v0, /device:TPU:1, one launch (start us, length us, event | category | flops | bytes accessed | tf_op | source)
XLA Modules:
  0.0 1662.4 jit_solution(8427986229018312662)
XLA Ops:
  25.7 29.2 %fusion.54 = (f32[8,1,16384]{2,1,0:T(1,128)S(1)}, f32[8,1,16384]{2,1,0:T(1,128)}, f32[8,1,16384]{2,1,0:T(1,128)}, f32[8,1,16384]{2,1,0:T(1,128)}, f32[8,1,16384]...) fusion(f32[8,8,16384]{2,1,0:T(8,128)} %get-tuple-element.77, ...), kind=kLoop, calls=%fused_computation.366 | loop fusion | bytes 16777216 | tf_op jit(solution)/shard_map/slice | solution.py:57
  92.8 17.5 %copy.189 = f32[3,16,16,256]{0,3,2,1:T(8,128)} copy(f32[3,16,16,256]{3,2,1,0:T(8,128)} %fusion.4) | data formatting | bytes 1572864 | tf_op jit(solution)/shard_map/add | solution.py:114
  110.4 38.5 %gather_fusion = f32[8192,3]{1,0:T(8,128)} fusion(f32[3,65536]{0,1:T(8,128)} %bitcast.608, s32[8192]{0:T(1024)S(1)} %broadcast_clamp_fusion), kind=kCustom, calls=%fused_computation | custom fusion | bytes 229376 | tf_op jit(solution)/shard_map/gather | solution.py:116
  253.2 61.6 %scatter_fusion.1 = f32[3,65536]{0,1:T(8,128)} fusion(f32[3,65536]{0,1:T(8,128)} %bitcast.609, s32[8192]{0:T(1024)S(1)} %bitcast.773, f32[8192,3]{1,0:T(8,128)} %copy.199), kind=kCustom, calls=%fused_computation.9 | custom fusion | flops 24576 | bytes 327680 | tf_op jit(solution)/shard_map/scatter-add | solution.py:138
  314.8 53.3 %slice_reduce_fusion.8 = (f32[65536]{0:T(1024)}, f32[65536]{0:T(1024)}, f32[65536]{0:T(1024)}) fusion(f32[3,65536]{0,1:T(8,128)} %scatter_fusion.1), kind=kLoop, calls=%fused_computation.24 | loop fusion | bytes 1572864 | tf_op jit(solution)/shard_map/slice | solution.py:40
  368.1 39.7 %slice_reduce_fusion.14 = (f32[61440]{0:T(1024)}, f32[61440]{0:T(1024)}) fusion(f32[3,65536]{0,1:T(8,128)} %scatter_fusion.1), kind=kLoop, calls=%fused_computation.30 | loop fusion | bytes 983040 | tf_op jit(solution)/shard_map/slice | solution.py:23
  441.8 18.3 %copy.202 = f32[3,65536]{1,0:T(4,128)} copy(f32[3,65536]{0,1:T(8,128)} %scatter_fusion.1) | data formatting | bytes 1572864 | tf_op jit(solution)/shard_map/scatter-add | solution.py:138
  517.4 38.4 %gather_fusion.2 = f32[8192,3]{1,0:T(8,128)} fusion(f32[3,65536]{0,1:T(8,128)} %copy.210, s32[8192]{0:T(1024)S(1)} %copy-done.120), kind=kCustom, calls=%fused_computation.2 | custom fusion | bytes 229376 | tf_op jit(solution)/shard_map/gather | solution.py:116
  609.5 24.1 %multiply_add_fusion.5 = (f32[1,8,8,16384]{3,2,1,0:T(8,128)}, f32[1,8,8,16384]{3,2,1,0:T(8,128)}, f32[1,8,8,16384]{3,2,1,0:T(8,128)}) fusion(f32[8,16384]{1,0:T(8,128)} %bitcast.679, f32[8,16384]{1,0:T(8,128)} %get-tuple-element.160, f32[8,16384]{1,0:T(8,128)} %bitcast.681, f32[8,16384]{1,0:T(8,128)} %get-tuple-element.161, f32[8,16384]{1,0:T(8,128)} %bitcast.683, ...), kind=kLoop, calls=%fused_computation.37 | loop fusion | flops 119537664 | bytes 46269696 | tf_op jit(solution)/shard_map/add | solution.py:71
  633.7 22.9 %multiply_add_fusion.10 = (f32[8,8,16384]{2,1,0:T(8,128)}, f32[8,8,16384]{2,1,0:T(8,128)S(1)}, f32[8,8,16384]{2,1,0:T(8,128)}) fusion(f32[8,8]{1,0:T(8,128)S(1)} %get-tuple-element.297, f32[8]{0:T(128)} %get-tuple-element.282, f32[8,16384]{1,0:T(8,128)} %bitcast.680, f32[8,16384]{1,0:T(8,128)} %get-tuple-element.160, f32[8]{0:T(128)} %get-tuple-element.37, ...), kind=kLoop, calls=%fused_computation.45 | loop fusion | flops 81788928 | bytes 42075392 | tf_op jit(solution)/shard_map/add | solution.py:71
  707.8 61.6 %scatter_fusion.3 = f32[3,65536]{0,1:T(8,128)} fusion(f32[3,65536]{0,1:T(8,128)} %copy.210, s32[8192]{0:T(1024)} %bitcast.772, f32[8192,3]{1,0:T(8,128)} %copy.211), kind=kCustom, calls=%fused_computation.11 | custom fusion | flops 24576 | bytes 327680 | tf_op jit(solution)/shard_map/scatter-add | solution.py:138
  769.4 53.3 %slice_reduce_fusion.5 = (f32[65536]{0:T(1024)}, f32[65536]{0:T(1024)}, f32[65536]{0:T(1024)}) fusion(f32[3,65536]{0,1:T(8,128)} %scatter_fusion.3), kind=kLoop, calls=%fused_computation.21 | loop fusion | bytes 1572864 | tf_op jit(solution)/shard_map/slice | solution.py:40
  822.6 39.7 %slice_reduce_fusion.12 = (f32[61440]{0:T(1024)}, f32[61440]{0:T(1024)}) fusion(f32[3,65536]{0,1:T(8,128)} %scatter_fusion.3), kind=kLoop, calls=%fused_computation.28 | loop fusion | bytes 983040 | tf_op jit(solution)/shard_map/slice | solution.py:23
  897.0 18.3 %copy.214 = f32[3,65536]{1,0:T(4,128)} copy(f32[3,65536]{0,1:T(8,128)} %scatter_fusion.3) | data formatting | bytes 1572864 | tf_op jit(solution)/shard_map/scatter-add | solution.py:138
  972.9 41.1 %gather_fusion.4 = f32[8192,3]{1,0:T(8,128)} fusion(f32[3,65536]{0,1:T(8,128)} %copy.222, s32[8192]{0:T(1024)} %copy-done.119), kind=kCustom, calls=%fused_computation.4 | custom fusion | bytes 229376 | tf_op jit(solution)/shard_map/gather | solution.py:116
  1077.3 25.5 %multiply_add_fusion.9 = (f32[8,8,16384]{2,1,0:T(8,128)}, f32[8,8,16384]{2,1,0:T(8,128)}) fusion(f32[8,8,16384]{2,1,0:T(8,128)} %get-tuple-element.56, f32[8,16384]{1,0:T(8,128)} %bitcast.647, f32[8,16384]{1,0:T(8,128)} %get-tuple-element.144, f32[8,16384]{1,0:T(8,128)} %bitcast.649, f32[8,16384]{1,0:T(8,128)} %get-tuple-element.145, ...), kind=kLoop, calls=%fused_computation.42 | loop fusion | flops 119537664 | bytes 50529280 | tf_op jit(solution)/shard_map/add | solution.py:71
  1166.5 61.4 %scatter_fusion.5 = f32[3,65536]{0,1:T(8,128)} fusion(f32[3,65536]{0,1:T(8,128)} %copy.222, s32[8192]{0:T(1024)S(1)} %bitcast.774, f32[8192,3]{1,0:T(8,128)} %copy.223), kind=kCustom, calls=%fused_computation.13 | custom fusion | flops 24576 | bytes 327680 | tf_op jit(solution)/shard_map/scatter-add | solution.py:138
  1228.0 53.3 %slice_reduce_fusion.2 = (f32[65536]{0:T(1024)}, f32[65536]{0:T(1024)S(1)}, f32[65536]{0:T(1024)S(1)}) fusion(f32[3,65536]{0,1:T(8,128)} %scatter_fusion.5), kind=kLoop, calls=%fused_computation.18 | loop fusion | bytes 1572864 | tf_op jit(solution)/shard_map/slice | solution.py:40
  1281.3 39.7 %slice_reduce_fusion.10 = (f32[61440]{0:T(1024)}, f32[61440]{0:T(1024)}) fusion(f32[3,65536]{0,1:T(8,128)} %scatter_fusion.5), kind=kLoop, calls=%fused_computation.26 | loop fusion | bytes 983040 | tf_op jit(solution)/shard_map/slice | solution.py:23
  1345.0 18.3 %copy.226 = f32[3,65536]{1,0:T(4,128)} copy(f32[3,65536]{0,1:T(8,128)} %scatter_fusion.5) | data formatting | bytes 1572864 | tf_op jit(solution)/shard_map/scatter-add | solution.py:138
  1413.1 38.4 %gather_fusion.6 = f32[8192,3]{1,0:T(8,128)} fusion(f32[3,65536]{0,1:T(8,128)} %copy.234, s32[8192]{0:T(1024)S(1)} %copy-done.121), kind=kCustom, calls=%fused_computation.6 | custom fusion | bytes 229376 | tf_op jit(solution)/shard_map/gather | solution.py:116
  1528.2 33.7 %multiply_add_fusion.1 = (f32[1,8,8,16384]{3,2,1,0:T(8,128)S(1)}, f32[1,8,8,16384]{3,2,1,0:T(8,128)S(1)}, f32[1,8,8,16384]{3,2,1,0:T(8,128)S(1)}) fusion(f32[8,16384]{1,0:T(8,128)} %bitcast.728, f32[8,16384]{1,0:T(8,128)} %copy-done.33, f32[8,16384]{1,0:T(8,128)} %bitcast.730, f32[8,16384]{1,0:T(8,128)} %copy-done.34, f32[8,16384]{1,0:T(8,128)} %bitcast.732, ...), kind=kLoop, calls=%fused_computation.33 | loop fusion | flops 159383552 | bytes 58918144 | tf_op jit(solution)/shard_map/add | solution.py:71
  1580.5 61.4 %scatter_fusion.7 = f32[3,65536]{0,1:T(8,128)} fusion(f32[3,65536]{0,1:T(8,128)} %copy.234, s32[8192]{0:T(1024)S(1)} %bitcast.775, f32[8192,3]{1,0:T(8,128)} %copy.235), kind=kCustom, calls=%fused_computation.15 | custom fusion | flops 24576 | bytes 327680 | tf_op jit(solution)/shard_map/scatter-add | solution.py:138
  1642.0 20.2 %copy.236 = f32[3,16,16,256]{3,2,1,0:T(8,128)} copy(f32[3,16,16,256]{0,3,2,1:T(8,128)} %bitcast.614) | data formatting | bytes 1572864
  (677 shorter events, 749.3 us)
Async XLA Ops:
  2.2 75.7 %collective-permute-start = (f32[2,16,1,256]{3,2,1,0:T(1,128)}, f32[2,16,1,256]{3,2,1,0:T(1,128)}, u32[]{:S(2)}, u32[]{:S(2)}) collective-permute-start(f32[2,16,1,256]{3,2,1,0:T(1,128)} %slice.1091), channel_id=1, source_target_pairs={{1,0},{2,1},{3,2},{4,3},{5,4},{6,5},{7,6},{9,8},{10,9},{11,10},{12... | collective-permute-start | bytes 98312 | tf_op jit(solution)/shard_map/ppermute | solution.py:17
  4.9 73.7 %collective-permute-start.1 = (f32[2,1,16,256]{3,2,1,0:T(8,128)}, f32[2,1,16,256]{3,2,1,0:T(8,128)}, u32[]{:S(2)}, u32[]{:S(2)}) collective-permute-start(f32[2,1,16,256]{3,2,1,0:T(8,128)} %slice.1099), channel_id=1, source_target_pairs={{8,0},{16,8},{24,16},{32,24},{40,32},{48,40},{56,48},{64,56},{72,6... | collective-permute-start | bytes 98312 | tf_op jit(solution)/shard_map/ppermute | solution.py:17
  80.7 10.1 collective-permute-start.2
  87.0 4.4 collective-permute-start.3
  172.7 24.4 %all-to-all-start = ((f32[3,128,128]{2,0,1:T(4,128)}), f32[3,128,128]{2,0,1:T(4,128)}, u32[]{:S(2)}, u32[]{:S(2)}) async-start(f32[3,128,128]{2,0,1:T(4,128)} %copy.194), calls=%async_computation | async-start | bytes 524288 | tf_op jit(solution)/shard_map/all_to_all | solution.py:122
  214.4 23.8 %all-to-all-start.1 = ((f32[3,128,128]{2,0,1:T(4,128)}), f32[3,128,128]{2,0,1:T(4,128)}, u32[]{:S(2)}, u32[]{:S(2)}) async-start(f32[3,128,128]{2,0,1:T(4,128)} %multiply_bitcast_fusion.3), calls=%async_computation.1 | async-start | bytes 524288 | tf_op jit(solution)/shard_map/all_to_all | solution.py:128
  427.5 47.3 %collective-permute-start.4 = (f32[2,16,1,256]{3,2,1,0:T(1,128)S(1)}, f32[2,16,1,256]{3,2,1,0:T(1,128)}, u32[]{:S(2)}, u32[]{:S(2)}) collective-permute-start(f32[2,16,1,256]{3,2,1,0:T(1,128)S(1)} %copy.301), channel_id=1, source_target_pairs={{1,0},{2,1},{3,2},{4,3},{5,4},{6,5},{7,6},{9,8},{10,9},{11,10},{12... | collective-permute-start | bytes 98312 | tf_op jit(solution)/shard_map/ppermute | solution.py:17
  462.9 12.6 collective-permute-start.5
  481.0 8.9 collective-permute-start.6
  487.0 3.8 collective-permute-start.7
  579.6 27.5 %all-to-all-start.2 = ((f32[3,128,128]{2,0,1:T(4,128)}), f32[3,128,128]{2,0,1:T(4,128)}, u32[]{:S(2)}, u32[]{:S(2)}) async-start(f32[3,128,128]{2,0,1:T(4,128)} %copy.206), calls=%async_computation.2 | async-start | bytes 524288 | tf_op jit(solution)/shard_map/all_to_all | solution.py:122
  658.3 34.5 %all-to-all-start.3 = ((f32[3,128,128]{2,0,1:T(4,128)}), f32[3,128,128]{2,0,1:T(4,128)}, u32[]{:S(2)}, u32[]{:S(2)}) async-start(f32[3,128,128]{2,0,1:T(4,128)} %multiply_bitcast_fusion.2), calls=%async_computation.3 | async-start | bytes 524288 | tf_op jit(solution)/shard_map/all_to_all | solution.py:128
  882.7 47.2 %collective-permute-start.8 = (f32[2,16,1,256]{3,2,1,0:T(1,128)}, f32[2,16,1,256]{3,2,1,0:T(1,128)}, u32[]{:S(2)}, u32[]{:S(2)}) collective-permute-start(f32[2,16,1,256]{3,2,1,0:T(1,128)} %copy.303), channel_id=1, source_target_pairs={{1,0},{2,1},{3,2},{4,3},{5,4},{6,5},{7,6},{9,8},{10,9},{11,10},{12... | collective-permute-start | bytes 98312 | tf_op jit(solution)/shard_map/ppermute | solution.py:17
  918.1 12.7 collective-permute-start.9
  936.5 8.9 collective-permute-start.10
  942.3 4.0 collective-permute-start.11
  1037.9 36.5 %all-to-all-start.4 = ((f32[3,128,128]{2,0,1:T(4,128)}), f32[3,128,128]{2,0,1:T(4,128)}, u32[]{:S(2)}, u32[]{:S(2)}) async-start(f32[3,128,128]{2,0,1:T(4,128)} %copy.218), calls=%async_computation.4 | async-start | bytes 524288 | tf_op jit(solution)/shard_map/all_to_all | solution.py:122
  1135.1 27.2 %all-to-all-start.5 = ((f32[3,128,128]{2,0,1:T(4,128)}), f32[3,128,128]{2,0,1:T(4,128)S(1)}, u32[]{:S(2)}, u32[]{:S(2)}) async-start(f32[3,128,128]{2,0,1:T(4,128)} %multiply_bitcast_fusion.1), calls=%async_computation.5 | async-start | bytes 524288 | tf_op jit(solution)/shard_map/all_to_all | solution.py:128
  1336.8 38.9 %collective-permute-start.12 = (f32[2,16,1,256]{3,2,1,0:T(1,128)S(1)}, f32[2,16,1,256]{3,2,1,0:T(1,128)}, u32[]{:S(2)}, u32[]{:S(2)}) collective-permute-start(f32[2,16,1,256]{3,2,1,0:T(1,128)S(1)} %copy.305), channel_id=1, source_target_pairs={{1,0},{2,1},{3,2},{4,3},{5,4},{6,5},{7,6},{9,8},{10,9},{11,10},{12... | collective-permute-start | bytes 98312 | tf_op jit(solution)/shard_map/ppermute | solution.py:17
  1366.2 10.2 collective-permute-start.13
  1381.6 8.9 collective-permute-start.14
  1387.6 3.9 collective-permute-start.15
  1459.9 27.1 %all-to-all-start.6 = ((f32[3,128,128]{2,0,1:T(4,128)}), f32[3,128,128]{2,0,1:T(4,128)}, u32[]{:S(2)}, u32[]{:S(2)}) async-start(f32[3,128,128]{2,0,1:T(4,128)} %copy.230), calls=%async_computation.6 | async-start | bytes 524288 | tf_op jit(solution)/shard_map/all_to_all | solution.py:122
  1517.9 58.5 %all-to-all-start.7 = ((f32[3,128,128]{2,0,1:T(4,128)}), f32[3,128,128]{2,0,1:T(4,128)S(1)}, u32[]{:S(2)}, u32[]{:S(2)}) async-start(f32[3,128,128]{2,0,1:T(4,128)} %multiply_bitcast_fusion), calls=%async_computation.7 | async-start | bytes 524288 | tf_op jit(solution)/shard_map/all_to_all | solution.py:128
  (165 other events, 2367.0 us)
where the time goes:
time: 1680 us; the launch traced here: 1660 us
  local copies, waits for them, and re-layouts  1040 us (62%)
  other arithmetic  454 us (27%)
  starting transfers between devices  148 us (9%)
    scatter-add x4, other arithmetic, body(): flattened = flattened.at[:, positions].add(-back_terms)  246 us
    slice x3, local copies, waits for them, and re-layouts, curl_ahead(): fields[2]  160 us
    gather x4, local copies, waits for them, and re-layouts, body(): samples = flattened[:, positions].reshape(3, tile_count, per_tile)  156 us
    slice x19, local copies, waits for them, and re-layouts, forward(): lax.slice_in_dim(values_in, 1, length, axis=along)  138 us
    unnamed x406, local copies, waits for them, and re-layouts  114 us
    slice x7, local copies, waits for them, and re-layouts, commutator(): matrix[:, inner][:, None, :] * symmetric[inner][None, :, None]  93.7 us
    add x3, other arithmetic, advance_driven(): real_part + time_step * change_real  80.8 us
    add x4, local copies, waits for them, and re-layouts, body(): field_e + courant * curl_behind(field_h, behind_planes, behind_rows)  66.3 us
  transfers between devices with their start and end apart: 24, of which 5 were waited for; matrix products, arithmetic and copies ran while one was open for 21% of the time, Pallas kernels for 0%

commit v1 on v0

v1 whole, which is shorter than its diff:
```python
import functools

import jax
import jax.numpy as jnp
from jax import lax
from jax.experimental import pallas as pl
from jax.experimental.pallas import tpu as pltpu
from jax.sharding import PartitionSpec as P

TILE = 128
STEPS = 4
COURANT = 0.5
TIME_STEP = 0.12

MESH = pl.DeviceIdType.MESH
F32 = jnp.float32
BF16 = jnp.bfloat16


def iota(shape, axis):
    return lax.broadcasted_iota(jnp.int32, shape, axis)


def lanes_at(values, index):
    return jnp.take_along_axis(values, index, axis=1, mode="promise_in_bounds")


def split(values):
    high = values.astype(BF16)
    return high, (values - high.astype(F32)).astype(BF16)


def product(left, right):
    return jnp.dot(left, right, preferred_element_type=F32)


def exact(left, right):
    return jnp.dot(left, right, preferred_element_type=F32, precision=lax.Precision.HIGHEST)


def exact_t(left, right):
    return lax.dot_general(
        left,
        right,
        (((1,), (1,)), ((), ())),
        preferred_element_type=F32,
        precision=lax.Precision.HIGHEST,
    )


def shift_rows(values, amount):
    return pltpu.roll(values, amount % values.shape[0], 0)


def shift_lanes(values, amount):
    return pltpu.roll(values, amount % values.shape[1], 1)


def level_constants(levels, coupling, rates, size):
    pairs = size * size
    first = jnp.where(iota((pairs, size), 0) // size == iota((pairs, size), 1), 1.0, 0.0).astype(F32)
    second = jnp.where(iota((pairs, size), 0) % size == iota((pairs, size), 1), 1.0, 0.0).astype(F32)
    row_at, col_at = iota((pairs, pairs), 0), iota((pairs, pairs), 1)
    eye = jnp.where(row_at == col_at, 1.0, 0.0).astype(F32)

    def pair_of(pick):
        half = exact(pick, coupling)
        return 0.5 * (exact_t(half, pick) + exact_t(pick, half))

    def symmetrized(values):
        return 0.5 * (
            jnp.sum(exact(first, values) * second, axis=1, keepdims=True)
            + jnp.sum(exact(second, values) * first, axis=1, keepdims=True)
        )

    def as_row(column):
        return jnp.sum(eye * column, axis=0, keepdims=True)

    commute = jnp.where(row_at % size == col_at % size, pair_of(first), 0.0) - jnp.where(
        row_at // size == col_at // size, pair_of(second), 0.0
    )
    sym = symmetrized(coupling)
    off_diagonal = jnp.where(
        iota((pairs, 1), 0) // size == iota((pairs, 1), 0) % size, 0.0, 1.0
    ).astype(F32)
    decay = TIME_STEP * symmetrized(rates) * off_diagonal
    spacing = TIME_STEP * jnp.sum((first - second) * levels, axis=1, keepdims=True)

    sym_row, decay_row, spacing_row = as_row(sym), as_row(decay), as_row(spacing)
    rows = iota((8, pairs), 0)

    def free(real, imag):
        keep = 1.0 - decay_row
        return real * keep - imag * spacing_row, real * spacing_row + imag * keep

    def driven(real, imag):
        return -exact(imag, commute), exact(real, commute)

    def both(real, imag, distance):
        free_real, free_imag = free(real, imag)
        driven_real, driven_imag = driven(real, imag)
        return (
            free_real + shift_rows(driven_real, distance),
            free_imag + shift_rows(driven_imag, distance),
        )

    push = exact(jnp.broadcast_to(sym_row, (8, pairs)), commute)
    real_zero = jnp.where(rows == 0, -sym_row * decay_row, 0.0)
    imag_zero = jnp.where(rows == 0, sym_row * spacing_row, jnp.where(rows == 1, push, 0.0))
    real_one, imag_one = both(real_zero, imag_zero, 2)
    real_two, imag_two = both(real_one, imag_one, 4)

    def parts(matrix):
        high, low = split(matrix)
        return jnp.concatenate([high, high, low], axis=1)

    begin = parts(
        jnp.concatenate(
            [real_one + shift_rows(real_zero, 4), imag_one + shift_rows(imag_zero, 4)], axis=0
        )
    )
    later = parts(jnp.concatenate([commute, real_two, imag_two], axis=0))
    keep = jnp.broadcast_to(1.0 - decay, (pairs, TILE))
    spacing = jnp.broadcast_to(spacing, (pairs, TILE))
    return begin, later, keep, spacing


def kernel(
    gx,
    gy,
    cx,
    cy,
    levels_in,
    coupling_in,
    rates_in,
    cells_in,
    owner_in,
    offsets_in,
    e_in,
    h_in,
    dens_in,
    dip_in,
    e_out,
    h_out,
    dens_out,
    dens,
    dip_mine,
    pick,
    unpick,
    off_ref,
    perm_ref,
    last_ref,
    some_ref,
    same_ref,
    begin_ref,
    later_ref,
    keep_ref,
    spacing_ref,
    ep,
    hp,
    row_e,
    row_h,
    halo_e,
    halo_h,
    dip_send,
    dip_recv,
    drive_send,
    drive_recv,
    coef_send,
    coef_recv,
    coef_next,
    halo_send,
    halo_recv,
    dip_sems,
    drive_ssem,
    drive_rsem,
    coef_ssem,
    coef_rsem,
    in_sem,
    out_sem,
    field_sem,
):
    mx = lax.axis_index("gx")
    my = lax.axis_index("gy")
    me = mx * gy + my
    count = gx * gy
    plane = cy
    cols = cx * cy
    nz = 2 * TILE
    group = gy * TILE
    size = levels_in.shape[1]
    pairs = size * size

    def load_group(g):
        part = pl.ds(pl.multiple_of(g * group, group), group)
        return pltpu.make_async_copy(dens_in.at[:, part], dens.at[:, part], in_sem.at[g])

    def store_group(g):
        part = pl.ds(pl.multiple_of(g * group, group), group)
        return pltpu.make_async_copy(dens.at[:, part], dens_out.at[:, part], out_sem.at[g])

    field_loads = (
        pltpu.make_async_copy(e_in, ep.at[:, 0:cols, :], field_sem.at[0]),
        pltpu.make_async_copy(h_in, hp.at[:, plane : plane + cols, :], field_sem.at[1]),
    )
    field_stores = (
        pltpu.make_async_copy(ep.at[:, 0:cols, :], e_out, field_sem.at[0]),
        pltpu.make_async_copy(hp.at[:, plane : plane + cols, :], h_out, field_sem.at[1]),
    )
    dip_load = pltpu.make_async_copy(dip_in, dip_mine, field_sem.at[2])

    def along_x(j):
        return lax.rem(mx + j, gx)

    def along_y(j):
        return lax.rem(my + j, gy)

    def device_of(number):
        return number // gy, lax.rem(number, gy)

    def to_all(source, target, base, step_of, width, send_sem, recv_sem):
        def one(j, carry):
            peer = lax.rem(me + j, count)
            pltpu.make_async_remote_copy(
                src_ref=source.at[pl.ds(base + peer * step_of, width), :],
                dst_ref=target.at[pl.ds(base + me * step_of, width), :],
                send_sem=send_sem,
                recv_sem=recv_sem,
                device_id=device_of(peer),
                device_id_type=MESH,
            ).start()
            return carry

        lax.fori_loop(1, count, one, 0, unroll=8)
        own = pl.ds(base + me * step_of, width)
        target[own, :] = source[own, :]

    def whole(source, target, base, width, send_sem, recv_sem):
        rows = pl.ds(base, (count - 1) * width)
        return pltpu.make_async_remote_copy(
            src_ref=source.at[rows, :],
            dst_ref=target.at[rows, :],
            send_sem=send_sem,
            recv_sem=recv_sem,
            device_id=(along_x(1), my),
            device_id_type=MESH,
        )

    def all_drive(step):
        return whole(
            drive_send, drive_recv, step * count, 1, drive_ssem.at[step], drive_rsem.at[step]
        )

    def all_coef(step):
        return whole(
            coef_send, coef_recv, step * 2 * count, 2, coef_ssem.at[step], coef_rsem.at[step]
        )

    all_dip = whole(dip_send, dip_recv, 0, 4, dip_sems.at[0], dip_sems.at[1])

    x_below, x_above = along_x(gx - 1), along_x(1)
    y_below, y_above = along_y(gy - 1), along_y(1)

    def halo_copy(which, source, target, device):
        return pltpu.make_async_remote_copy(
            src_ref=source,
            dst_ref=target,
            send_sem=halo_send.at[which],
            recv_sem=halo_recv.at[which],
            device_id=device,
            device_id_type=MESH,
        )

    e_plane = halo_copy(
        0, ep.at[1:3, 0:plane, :], ep.at[1:3, cols : cols + plane, :], (x_below, my)
    )
    e_row = halo_copy(1, row_e, halo_e, (mx, y_below))
    h_plane = halo_copy(
        2, hp.at[1:3, cols : cols + plane, :], hp.at[1:3, 0:plane, :], (x_above, my)
    )
    h_row = halo_copy(3, row_h, halo_h, (mx, y_above))

    def send_e():
        for x in range(cx):
            row_e[0, x : x + 1, :] = ep[0, x * plane : x * plane + 1, :]
            row_e[1, x : x + 1, :] = ep[2, x * plane : x * plane + 1, :]
        e_row.start()
        e_plane.start()

    for copy in field_loads:
        copy.start()
    dip_load.start()

    @pl.loop(0, gx)
    def _(g):
        load_group(g).start()

    barrier = pltpu.get_barrier_semaphore()

    def greet(j, carry):
        pl.semaphore_signal(
            barrier, inc=1, device_id=device_of(lax.rem(me + j, count)), device_id_type=MESH
        )
        return carry

    lax.fori_loop(1, count, greet, 0, unroll=8)

    dip_load.wait()

    def dip_row(s, carry):
        lanes = pl.ds(pl.multiple_of(s * TILE, TILE), TILE)
        dip_send[pl.ds(pl.multiple_of(s * 4, 4), 3), :] = dip_mine[:, lanes]
        return carry

    dip_send[pl.ds(3, count, stride=4), :] = jnp.zeros((count, TILE), F32)
    lax.fori_loop(0, count, dip_row, 0, unroll=8)
    for copy in field_loads:
        copy.wait()

    pl.semaphore_wait(barrier, count - 1)
    send_e()
    to_all(dip_send, dip_recv, 0, 4, 4, dip_sems.at[0], dip_sems.at[1])

    begin, later, keep, spacing = level_constants(
        levels_in[...], coupling_in[...], rates_in[...], size
    )
    begin_ref[...] = begin
    later_ref[...] = later
    keep_ref[...] = keep
    spacing_ref[...] = spacing

    def stacked(real, imag):
        real_high, real_low = split(real)
        imag_high, imag_low = split(imag)
        high = jnp.concatenate([real_high, imag_high], axis=1)
        low = jnp.concatenate([real_low, imag_low], axis=1)
        return jnp.concatenate([high, low, high], axis=0)

    @pl.loop(0, gx)
    def _(g):
        load_group(g).wait()

    def first_look(s, carry):
        part = pl.ds(pl.multiple_of(s * TILE, TILE), TILE)
        seen = product(begin_ref[...], stacked(dens[0:pairs, part], dens[pairs : 2 * pairs, part]))
        coef_next[pl.ds(pl.multiple_of(s * 8, 8), 8), :] = seen[0:8, 0:TILE] + seen[8:16, TILE:]
        return carry

    lax.fori_loop(0, count, first_look, 0, unroll=4)

    def send_coef(step, alpha, beta):
        base = step * 2 * count
        coef_send[pl.ds(base, count, stride=2), :] = alpha
        coef_send[pl.ds(base + 1, count, stride=2), :] = beta
        to_all(coef_send, coef_recv, base, 2, 2, coef_ssem.at[step], coef_rsem.at[step])

    send_coef(
        0, coef_next[pl.ds(4, count, stride=8), :], coef_next[pl.ds(5, count, stride=8), :]
    )

    lane = iota((count, TILE), 1)
    sub = iota((count, TILE), 0)

    def find_places():
        eye = jnp.where(lane == sub, 1.0, 0.0).astype(F32)

        def column_of(row):
            return jnp.sum(eye * row, axis=1, keepdims=True)

        owner_row = owner_in[...].astype(F32)
        owner_col = column_of(owner_row)
        tiles = cells_in[...]
        cell_row = ((tiles & 1) * cols + (tiles >> 1)).astype(F32)
        cell_col = column_of(cell_row)
        alike = jnp.where(owner_col == owner_row, 1.0, 0.0)
        rank_col = jnp.sum(jnp.where(lane < sub, alike, 0.0), axis=1, keepdims=True)
        rank_row = jnp.sum(jnp.where(sub < lane, alike, 0.0), axis=0, keepdims=True)

        def flags(condition):
            return jnp.where(condition, 1.0, 0.0).astype(BF16)

        named = owner_row == sub.astype(F32)
        slot_zero = flags(named & (rank_row == 0.0))
        slot_one = flags(named & (rank_row == 1.0))
        taking = owner_col == lane.astype(F32)
        slot_zero_t = flags(taking & (rank_col == 0.0))
        slot_one_t = flags(taking & (rank_col == 1.0))
        at_cell = flags(cell_col == iota((count, 2 * cols), 1).astype(F32))
        at_cell_t = flags(cell_row == iota((2 * cols, count), 0).astype(F32))
        pick[0:count, :] = product(slot_zero, at_cell).astype(BF16)
        pick[count : 2 * count, :] = product(slot_one, at_cell).astype(BF16)
        unpick[:, 0:count] = product(at_cell_t, slot_zero_t).astype(BF16)
        unpick[:, count : 2 * count] = product(at_cell_t, slot_one_t).astype(BF16)

        offsets = offsets_in[...].astype(F32)
        offsets = jnp.concatenate([offsets, offsets], axis=1).astype(BF16)
        off = jnp.where(lane < TILE // 2, product(slot_zero, offsets), product(slot_one, offsets))
        off = off.astype(jnp.int32)
        off_ref[...] = off

        half = TILE // 2
        place = lane & (half - 1)
        base = lane & half
        key = off * half + place
        length = 2
        while length <= half:
            d = length // 2
            while d >= 1:
                partner = lanes_at(key, lane ^ d)
                lower = jnp.where((lane & d) == 0, 1, 0)
                upward = jnp.where((place & length) == 0, 1, 0)
                key = jnp.where(
                    lower == upward, jnp.minimum(key, partner), jnp.maximum(key, partner)
                )
                d //= 2
            length *= 2
        perm_ref[...] = base | (key & (half - 1))
        ordered = key >> 6
        d = 1
        level = 0
        while d < half:
            together = (place >= d) & (shift_lanes(ordered, d) == ordered)
            same_ref[level] = jnp.where(together, 1.0, 0.0).astype(F32)
            d *= 2
            level += 1
        for k in range(2):
            found = jnp.zeros((count, TILE), jnp.int32)
            jump = half // 2
            while jump >= 1:
                seen = lanes_at(ordered, found + (k * half + jump - 1))
                found = jnp.where(seen <= lane, found + jump, found)
                jump //= 2
            seen = lanes_at(ordered, found + k * half)
            found = jnp.where(seen <= lane, found + 1, found)
            last = jnp.maximum(found - 1, 0) + k * half
            hit = (found > 0) & (lanes_at(ordered, last) == lane)
            last_ref[k] = last
            some_ref[k] = jnp.where(hit, 1.0, 0.0).astype(F32)

    row_at = iota((plane, nz), 0)
    z_at = iota((plane, nz), 1)

    def next_y(values, row):
        return jnp.where(row_at == plane - 1, row, shift_rows(values, -1))

    def prior_y(values, row):
        return jnp.where(row_at == 0, row, shift_rows(values, 1))

    def next_z(values):
        return jnp.where(z_at == nz - 1, 0.0, shift_lanes(values, -1))

    def prior_z(values):
        return jnp.where(z_at == 0, 0.0, shift_lanes(values, 1))

    def step_h():
        keep_x = jnp.where(mx == gx - 1, 0.0, 1.0).astype(F32)
        keep_y = jnp.where(my == gy - 1, 0.0, 1.0).astype(F32)
        for c in (1, 2):
            ep[c, cols : cols + plane, :] = ep[c, cols : cols + plane, :] * keep_x
        for x in range(cx):
            here = slice(x * plane, (x + 1) * plane)
            after = slice((x + 1) * plane, (x + 2) * plane)
            e0, e1, e2 = ep[0, here, :], ep[1, here, :], ep[2, here, :]
            e1_x, e2_x = ep[1, after, :], ep[2, after, :]
            e0_y = next_y(e0, halo_e[0, x : x + 1, :] * keep_y)
            e2_y = next_y(e2, halo_e[1, x : x + 1, :] * keep_y)
            hp[0, after, :] = hp[0, after, :] - COURANT * ((e2_y - e2) - (next_z(e1) - e1))
            hp[1, after, :] = hp[1, after, :] - COURANT * ((next_z(e0) - e0) - (e2_x - e2))
            hp[2, after, :] = hp[2, after, :] - COURANT * ((e1_x - e1) - (e0_y - e0))
            bottom = slice((x + 2) * plane - 1, (x + 2) * plane)
            row_h[0, x : x + 1, :] = hp[0, bottom, :]
            row_h[1, x : x + 1, :] = hp[2, bottom, :]

    def step_e():
        hold_x = jnp.where(mx == 0, 0.0, 1.0).astype(F32)
        hold_y = jnp.where(my == 0, 0.0, 1.0).astype(F32)
        for c in (1, 2):
            hp[c, 0:plane, :] = hp[c, 0:plane, :] * hold_x
        for x in range(cx):
            here = slice(x * plane, (x + 1) * plane)
            after = slice((x + 1) * plane, (x + 2) * plane)
            h0, h1, h2 = hp[0, after, :], hp[1, after, :], hp[2, after, :]
            h1_x, h2_x = hp[1, here, :], hp[2, here, :]
            h0_y = prior_y(h0, halo_h[0, x : x + 1, :] * hold_y)
            h2_y = prior_y(h2, halo_h[1, x : x + 1, :] * hold_y)
            ep[0, here, :] = ep[0, here, :] + COURANT * ((h2 - h2_y) - (h1 - prior_z(h1)))
            ep[1, here, :] = ep[1, here, :] + COURANT * ((h0 - prior_z(h0)) - (h2 - h2_x))
            ep[2, here, :] = ep[2, here, :] + COURANT * ((h1 - h1_x) - (h0 - h0_y))

    def dipole_rows(c):
        return dip_recv[pl.ds(c, count, stride=4), :]

    def sampled_drive():
        drive = jnp.zeros((count, TILE), F32)
        for c in range(3):
            rows = jnp.zeros((2 * count, 2 * TILE), F32)
            for h in range(2):
                parts = jnp.concatenate(split(ep[c, 0:cols, h * TILE : (h + 1) * TILE]), axis=1)
                rows = rows + product(pick[:, h * cols : (h + 1) * cols], parts)
            rows = rows[:, 0:TILE] + rows[:, TILE : 2 * TILE]
            sample = jnp.where(
                lane < TILE // 2,
                lanes_at(rows[0:count], off_ref[...]),
                lanes_at(rows[count : 2 * count], off_ref[...]),
            )
            drive = drive + dipole_rows(c) * sample
        return drive * TIME_STEP

    def feed_field(moved):
        for c in range(3):
            sums = lanes_at(moved * dipole_rows(c), perm_ref[...])
            d = 1
            level = 0
            while d < TILE // 2:
                sums = sums + same_ref[level] * shift_lanes(sums, d)
                d *= 2
                level += 1
            rows = [lanes_at(sums, last_ref[k]) * some_ref[k] for k in range(2)]
            parts = jnp.concatenate(split(jnp.concatenate(rows, axis=0)), axis=1)
            change = product(unpick[...], parts)
            change = change[:, 0:TILE] + change[:, TILE : 2 * TILE]
            for h in range(2):
                part = slice(h * TILE, (h + 1) * TILE)
                ep[c, 0:cols, part] = ep[c, 0:cols, part] - change[h * cols : (h + 1) * cols, :]

    def advance(step, start, number):
        def one(i, carry):
            s = start + i
            part = pl.ds(pl.multiple_of(s * TILE, TILE), TILE)
            real = dens[0:pairs, part]
            imag = dens[pairs : 2 * pairs, part]
            force = drive_recv[pl.ds(step * count + s, 1), :]
            out = product(later_ref[...], stacked(real, imag))
            keep = keep_ref[...]
            spacing = spacing_ref[...]
            dens[0:pairs, part] = keep * real + spacing * imag + force * out[0:pairs, TILE:]
            dens[pairs : 2 * pairs, part] = (
                keep * imag - spacing * real - force * out[0:pairs, 0:TILE]
            )
            seen = out[pairs : pairs + 8, 0:TILE] + out[pairs + 8 : pairs + 16, TILE:]
            coef_next[pl.ds(pl.multiple_of(s * 8, 8), 8), :] = seen + force * shift_rows(seen, 4)
            return carry

        lax.fori_loop(0, number, one, 0, unroll=4)

    middle = count // 2

    def one_step(step, carry):
        @pl.when(step >= 2)
        def _():
            advance(step - 2, middle, count - middle)

        @pl.when(step >= 1)
        def _():
            all_drive(step - 1).wait_recv()
            force = drive_recv[pl.ds(pl.multiple_of((step - 1) * count, count), count), :]

            def coef(k):
                return coef_next[pl.ds(k, count, stride=8), :]

            send_coef(step, coef(0) + force * coef(2), coef(1) + force * coef(3))

        e_plane.wait_recv()
        e_row.wait_recv()
        step_h()
        h_row.start()
        h_plane.start()

        @pl.when(step == 0)
        def _():
            find_places()

        @pl.when(step >= 1)
        def _():
            advance(step - 1, 0, middle)

        e_plane.wait_send()
        e_row.wait_send()
        h_plane.wait_recv()
        h_row.wait_recv()
        step_e()

        @pl.when(step == 0)
        def _():
            all_dip.wait_recv()

        drive = sampled_drive()
        drive_send[pl.ds(pl.multiple_of(step * count, count), count), :] = drive
        to_all(
            drive_send,
            drive_recv,
            step * count,
            1,
            1,
            drive_ssem.at[step],
            drive_rsem.at[step],
        )
        h_plane.wait_send()
        h_row.wait_send()
        all_coef(step).wait_recv()
        base = step * 2 * count
        alpha = coef_recv[pl.ds(base, count, stride=2), :]
        beta = coef_recv[pl.ds(base + 1, count, stride=2), :]
        feed_field(alpha + drive * beta)

        @pl.when(step < STEPS - 1)
        def _():
            send_e()

        return carry

    lax.fori_loop(0, STEPS, one_step, 0)

    for copy in field_stores:
        copy.start()
    advance(STEPS - 2, middle, count - middle)
    all_drive(STEPS - 1).wait_recv()

    @pl.loop(0, gx)
    def _(g):
        advance(STEPS - 1, g * gy, gy)
        store_group(g).start()

    all_dip.wait_send()

    @pl.loop(0, STEPS)
    def _(step):
        all_drive(step).wait_send()
        all_coef(step).wait_send()

    for copy in field_stores:
        copy.wait()

    @pl.loop(0, gx)
    def _(g):
        store_group(g).wait()


def body(
    field_e,
    field_h,
    density,
    dipole,
    levels,
    coupling,
    rates,
    tile_cells,
    tile_owner,
    emitter_offsets,
):
    gx = lax.axis_size("gx")
    gy = lax.axis_size("gy")
    count = gx * gy
    _, cx, cy, nz = field_e.shape
    cols = cx * cy
    pairs = coupling.shape[0] ** 2
    columns = density.shape[3]

    vmem = pl.BlockSpec(memory_space=pltpu.VMEM)
    hbm = pl.BlockSpec(memory_space=pl.ANY)
    dma = pltpu.SemaphoreType.DMA
    tall = (count, TILE)
    e_out, h_out, dens_out = pl.pallas_call(
        functools.partial(kernel, gx, gy, cx, cy),
        out_shape=(
            jax.ShapeDtypeStruct((3, cols, nz), F32),
            jax.ShapeDtypeStruct((3, cols, nz), F32),
            jax.ShapeDtypeStruct((2 * pairs, columns), F32),
        ),
        in_specs=[vmem] * 6 + [hbm] * 4,
        out_specs=(hbm, hbm, hbm),
        scratch_shapes=[
            pltpu.VMEM((2 * pairs, columns), F32),
            pltpu.VMEM((3, columns), F32),
            pltpu.VMEM((2 * count, 2 * cols), BF16),
            pltpu.VMEM((2 * cols, 2 * count), BF16),
            pltpu.VMEM(tall, jnp.int32),
            pltpu.VMEM(tall, jnp.int32),
            pltpu.VMEM((2,) + tall, jnp.int32),
            pltpu.VMEM((2,) + tall, F32),
            pltpu.VMEM((6,) + tall, F32),
            pltpu.VMEM((16, 3 * pairs), BF16),
            pltpu.VMEM((pairs + 16, 3 * pairs), BF16),
            pltpu.VMEM((pairs, TILE), F32),
            pltpu.VMEM((pairs, TILE), F32),
            pltpu.VMEM((3, cols + cy, nz), F32),
            pltpu.VMEM((3, cols + cy, nz), F32),
            pltpu.VMEM((2, cx, nz), F32),
            pltpu.VMEM((2, cx, nz), F32),
            pltpu.VMEM((2, cx, nz), F32),
            pltpu.VMEM((2, cx, nz), F32),
            pltpu.VMEM((4 * count, TILE), F32),
            pltpu.VMEM((4 * count, TILE), F32),
            pltpu.VMEM((STEPS * count, TILE), F32),
            pltpu.VMEM((STEPS * count, TILE), F32),
            pltpu.VMEM((STEPS * 2 * count, TILE), F32),
            pltpu.VMEM((STEPS * 2 * count, TILE), F32),
            pltpu.VMEM((8 * count, TILE), F32),
            dma((4,)),
            dma((4,)),
            dma((2,)),
            dma((STEPS,)),
            dma((STEPS,)),
            dma((STEPS,)),
            dma((STEPS,)),
            dma((gx,)),
            dma((gx,)),
            dma((3,)),
        ],
        compiler_params=pltpu.CompilerParams(
            collective_id=0, has_side_effects=True, vmem_limit_bytes=48 * 1024 * 1024
        ),
    )(
        levels.reshape(1, -1),
        coupling,
        rates,
        tile_cells.reshape(1, -1),
        tile_owner.reshape(1, -1),
        emitter_offsets,
        field_e.reshape(3, cols, nz),
        field_h.reshape(3, cols, nz),
        density.reshape(2 * pairs, columns),
        dipole,
    )
    return (
        e_out.reshape(field_e.shape),
        h_out.reshape(field_h.shape),
        dens_out.reshape(density.shape),
    )


def solution(mesh):
    placed = (
        P(None, "gx", "gy", None),
        P(None, "gx", "gy", None),
        P(None, None, None, ("gx", "gy")),
        P(None, ("gx", "gy")),
        P(),
        P(),
        P(),
        P(("gx", "gy")),
        P(("gx", "gy"), None),
        P(("gx", "gy"), None),
    )
    return jax.shard_map(
        body,
        mesh=mesh,
        in_specs=placed,
        out_specs=(
            P(None, "gx", "gy", None),
            P(None, "gx", "gy", None),
            P(None, None, None, ("gx", "gy")),
        ),
        check_vma=False,
    )
```

time: 1680 us -> 152 us (0.09); the launches traced: 1660 us -> 151 us
  local copies, waits for them, and re-layouts: 1040 us -> 16.7 us
  other arithmetic: 454 us -> 0 us
  starting transfers between devices: 148 us -> 0 us
  Pallas kernels: 0 us -> 134 us
    slice x55 -> x0, local copies, waits for them, and re-layouts: 462 us -> none  [the longest x3 160 us: curl_ahead(): fields[2]]
    scatter-add x4 -> x0, other arithmetic: 246 us -> none  [body(): flattened = flattened.at[:, positions].add(-back_terms)]
    gather x8 -> x0, local copies, waits for them, and re-layouts: 163 us -> none  [the longest x4 156 us: body(): samples = flattened[:, positions].reshape(3, tile_count, per_tile)]
    add x15 -> x0, other arithmetic: 141 us -> none  [the longest x3 80.8 us: advance_driven(): real_part + time_step * change_real]
    pallas_call x0 -> x1, Pallas kernels: none -> 134 us  [body(): pl.pallas_call(functools.partial(kernel, gx, gy, cx, cy), out_shape=(jax....]
    unnamed x406 -> x20, local copies, waits for them, and re-layouts: 114 us -> 16.7 us
    all_to_all x8 -> x0, starting transfers between devices: 93.5 us -> none  [the longest x4 57.1 us: body(): lax.all_to_all(outgoing.reshape(3, devices, -1), ('gx', 'gy'), split_axis...]
    add x5 -> x0, local copies, waits for them, and re-layouts: 66.4 us -> none  [the longest x4 66.3 us: body(): field_e + courant * curl_behind(field_h, behind_planes, behind_rows)]
  transfers between devices with their start and end apart: 24 -> 0, of which waited for: 5 -> 0; matrix products, arithmetic and copies ran while one was open for 21% -> 0% of each run, Pallas kernels for 0% -> 0%
where the time goes in v1:
time: 152 us; the launch traced here: 151 us
  Pallas kernels  134 us (88%)
  local copies, waits for them, and re-layouts  16.7 us (11%)
    pallas_call x1, Pallas kernels, body(): pl.pallas_call(functools.partial(kernel, gx, gy, cx, cy), out_shape=(jax....  134 us
    unnamed x20, local copies, waits for them, and re-layouts  16.7 us

profile of v1, /device:TPU:1, one launch (start us, length us, event | category | flops | bytes accessed | tf_op | source)
XLA Modules:
  0.0 151.2 jit_solution(8353964640484479177)
XLA Ops:
  0.6 0.8 copy.13.offsets_in
  1.5 0.0 copy-start
  1.5 1.1 copy-done
  2.6 0.0 copy-start.1
  2.6 1.1 copy-done.1
  3.8 0.0 copy-start.2
  3.8 0.9 copy-done.2
  4.7 0.0 copy-start.3
  4.7 0.7 copy-done.3
  5.4 0.0 copy-start.4
  5.4 0.7 copy-done.4
  6.1 0.0 copy-start.5
  6.1 0.7 copy-done.5
  6.7 0.0 copy-start.6
  6.7 0.7 copy-done.6
  7.4 0.0 copy-start.7
  7.4 0.7 copy-done.7
  8.0 133.8 %shard_map.121 = (f32[3,256,256]{2,1,0:T(8,128)S(1)}, f32[3,256,256]{2,1,0:T(8,128)S(1)}, f32[128,16384]{1,0:T(8,128)}) custom-call(f32[1,8]{1,0:T(1,128)S(1)} %bitcast.13, f32[8,8]{1,0:T(8,128)S(1)} %copy-done.3, f32[8,8]{1,0:T(8,128)S(1)} %copy-done.4, s32[1,128]{1,0:T(1,128)S(1)} %bitcast.14, s32[1,128]{1,0:T(1,128)S(1)} %bitcast.15, ...), custom_call_target="tpu_custom_call" | custom-call | tf_op jit(solution)/shard_map/pallas_call | solution.py:663
  141.9 0.9 copy.17
  142.7 0.9 copy.18
  143.6 7.6 %copy.19 = f32[2,8,8,16384]{3,2,1,0:T(8,128)} copy(f32[2,8,8,16384]{3,2,1,0:T(8,128)} %bitcast.17) | data formatting | bytes 16777216
Async XLA Ops:
  1.5 1.1 copy-start
  2.6 1.1 copy-start.1
  3.8 0.9 copy-start.2
  4.7 0.7 copy-start.3
  5.4 0.7 copy-start.4
  6.1 0.7 copy-start.5
  6.7 0.7 copy-start.6
  7.4 0.7 copy-start.7

commit v2 on v1

--- a/solution.py
+++ b/solution.py
@@ -11,6 +11,8 @@
 STEPS = 4
 COURANT = 0.5
 TIME_STEP = 0.12
+WIDTH = 2
+UNROLL = 4
 
 MESH = pl.DeviceIdType.MESH
 F32 = jnp.float32
@@ -32,6 +34,14 @@
 
 def product(left, right):
     return jnp.dot(left, right, preferred_element_type=F32)
+
+
+def stacked(real, imag):
+    real_high, real_low = split(real)
+    imag_high, imag_low = split(imag)
+    high = jnp.concatenate([real_high, imag_high], axis=1)
+    low = jnp.concatenate([real_low, imag_low], axis=1)
+    return jnp.concatenate([high, low, high], axis=0)
 
 
 def exact(left, right):
@@ -130,20 +140,29 @@
     gy,
     cx,
     cy,
+    levels_hbm,
+    coupling_hbm,
+    rates_hbm,
+    cells_hbm,
+    owner_hbm,
+    offsets_hbm,
+    e_in,
+    h_in,
+    dens_in,
+    dip_in,
+    ep,
+    hp,
+    dens,
+    drive_recv,
+    later_ref,
+    keep_ref,
+    spacing_ref,
     levels_in,
     coupling_in,
     rates_in,
     cells_in,
     owner_in,
     offsets_in,
-    e_in,
-    h_in,
-    dens_in,
-    dip_in,
-    e_out,
-    h_out,
-    dens_out,
-    dens,
     dip_mine,
     pick,
     unpick,
@@ -153,11 +172,6 @@
     some_ref,
     same_ref,
     begin_ref,
-    later_ref,
-    keep_ref,
-    spacing_ref,
-    ep,
-    hp,
     row_e,
     row_h,
     halo_e,
@@ -165,7 +179,6 @@
     dip_send,
     dip_recv,
     drive_send,
-    drive_recv,
     coef_send,
     coef_recv,
     coef_next,
@@ -177,7 +190,7 @@
     coef_ssem,
     coef_rsem,
     in_sem,
-    out_sem,
+    small_sem,
     field_sem,
 ):
     mx = lax.axis_index("gx")
@@ -195,18 +208,23 @@
         part = pl.ds(pl.multiple_of(g * group, group), group)
         return pltpu.make_async_copy(dens_in.at[:, part], dens.at[:, part], in_sem.at[g])
 
-    def store_group(g):
-        part = pl.ds(pl.multiple_of(g * group, group), group)
-        return pltpu.make_async_copy(dens.at[:, part], dens_out.at[:, part], out_sem.at[g])
-
     field_loads = (
         pltpu.make_async_copy(e_in, ep.at[:, 0:cols, :], field_sem.at[0]),
         pltpu.make_async_copy(h_in, hp.at[:, plane : plane + cols, :], field_sem.at[1]),
     )
-    field_stores = (
-        pltpu.make_async_copy(ep.at[:, 0:cols, :], e_out, field_sem.at[0]),
-        pltpu.make_async_copy(hp.at[:, plane : plane + cols, :], h_out, field_sem.at[1]),
-    )
+    small_loads = [
+        pltpu.make_async_copy(source, target, small_sem.at[i])
+        for i, (source, target) in enumerate(
+            (
+                (levels_hbm, levels_in),
+                (coupling_hbm, coupling_in),
+                (rates_hbm, rates_in),
+                (cells_hbm, cells_in),
+                (owner_hbm, owner_in),
+                (offsets_hbm, offsets_in),
+            )
+        )
+    ]
     dip_load = pltpu.make_async_copy(dip_in, dip_mine, field_sem.at[2])
 
     def along_x(j):
@@ -216,11 +234,14 @@
         return lax.rem(my + j, gy)
 
     def device_of(number):
-        return number // gy, lax.rem(number, gy)
+        return number >> (gy.bit_length() - 1), number & (gy - 1)
+
+    def other(j):
+        return (me + j) & (count - 1)
 
     def to_all(source, target, base, step_of, width, send_sem, recv_sem):
         def one(j, carry):
-            peer = lax.rem(me + j, count)
+            peer = other(j)
             pltpu.make_async_remote_copy(
                 src_ref=source.at[pl.ds(base + peer * step_of, width), :],
                 dst_ref=target.at[pl.ds(base + me * step_of, width), :],
@@ -287,9 +308,11 @@
         e_row.start()
         e_plane.start()
 
+    for copy in small_loads:
+        copy.start()
+    dip_load.start()
     for copy in field_loads:
         copy.start()
-    dip_load.start()
 
     @pl.loop(0, gx)
     def _(g):
@@ -298,12 +321,20 @@
     barrier = pltpu.get_barrier_semaphore()
 
     def greet(j, carry):
-        pl.semaphore_signal(
-            barrier, inc=1, device_id=device_of(lax.rem(me + j, count)), device_id_type=MESH
-        )
+        pl.semaphore_signal(barrier, inc=1, device_id=device_of(other(j)), device_id_type=MESH)
         return carry
 
     lax.fori_loop(1, count, greet, 0, unroll=8)
+
+    for copy in small_loads:
+        copy.wait()
+    begin, later, keep, spacing = level_constants(
+        levels_in[...], coupling_in[...], rates_in[...], size
+    )
+    begin_ref[...] = begin
+    later_ref[...] = later
+    keep_ref[...] = keep
+    spacing_ref[...] = spacing
 
     dip_load.wait()
 
@@ -321,42 +352,25 @@
     send_e()
     to_all(dip_send, dip_recv, 0, 4, 4, dip_sems.at[0], dip_sems.at[1])
 
-    begin, later, keep, spacing = level_constants(
-        levels_in[...], coupling_in[...], rates_in[...], size
-    )
-    begin_ref[...] = begin
-    later_ref[...] = later
-    keep_ref[...] = keep
-    spacing_ref[...] = spacing
-
-    def stacked(real, imag):
-        real_high, real_low = split(real)
-        imag_high, imag_low = split(imag)
-        high = jnp.concatenate([real_high, imag_high], axis=1)
-        low = jnp.concatenate([real_low, imag_low], axis=1)
-        return jnp.concatenate([high, low, high], axis=0)
-
-    @pl.loop(0, gx)
-    def _(g):
-        load_group(g).wait()
-
-    def first_look(s, carry):
-        part = pl.ds(pl.multiple_of(s * TILE, TILE), TILE)
-        seen = product(begin_ref[...], stacked(dens[0:pairs, part], dens[pairs : 2 * pairs, part]))
-        coef_next[pl.ds(pl.multiple_of(s * 8, 8), 8), :] = seen[0:8, 0:TILE] + seen[8:16, TILE:]
-        return carry
-
-    lax.fori_loop(0, count, first_look, 0, unroll=4)
+    def look_first():
+        @pl.loop(0, gx)
+        def _(g):
+            load_group(g).wait()
+
+        def one(s, carry):
+            part = pl.ds(pl.multiple_of(s * TILE, TILE), TILE)
+            state = stacked(dens[0:pairs, part], dens[pairs : 2 * pairs, part])
+            seen = product(begin_ref[...], state)
+            coef_next[pl.ds(pl.multiple_of(s * 8, 8), 8), :] = seen[0:8, 0:TILE] + seen[8:16, TILE:]
+            return carry
+
+        lax.fori_loop(0, count, one, 0, unroll=4)
 
     def send_coef(step, alpha, beta):
         base = step * 2 * count
         coef_send[pl.ds(base, count, stride=2), :] = alpha
         coef_send[pl.ds(base + 1, count, stride=2), :] = beta
         to_all(coef_send, coef_recv, base, 2, 2, coef_ssem.at[step], coef_rsem.at[step])
-
-    send_coef(
-        0, coef_next[pl.ds(4, count, stride=8), :], coef_next[pl.ds(5, count, stride=8), :]
-    )
 
     lane = iota((count, TILE), 1)
     sub = iota((count, TILE), 0)
@@ -392,9 +406,14 @@
         unpick[:, 0:count] = product(at_cell_t, slot_zero_t).astype(BF16)
         unpick[:, count : 2 * count] = product(at_cell_t, slot_one_t).astype(BF16)
 
-        offsets = offsets_in[...].astype(F32)
-        offsets = jnp.concatenate([offsets, offsets], axis=1).astype(BF16)
-        off = jnp.where(lane < TILE // 2, product(slot_zero, offsets), product(slot_one, offsets))
+        offsets = offsets_in[...].astype(F32).astype(BF16)
+
+        def offsets_of(slot):
+            return lax.dot_general(
+                slot, offsets, (((1,), (1,)), ((), ())), preferred_element_type=F32
+            )
+
+        off = jnp.concatenate([offsets_of(slot_zero), offsets_of(slot_one)], axis=1)
         off = off.astype(jnp.int32)
         off_ref[...] = off
 
@@ -524,24 +543,37 @@
                 ep[c, 0:cols, part] = ep[c, 0:cols, part] - change[h * cols : (h + 1) * cols, :]
 
     def advance(step, start, number):
-        def one(i, carry):
-            s = start + i
-            part = pl.ds(pl.multiple_of(s * TILE, TILE), TILE)
-            real = dens[0:pairs, part]
-            imag = dens[pairs : 2 * pairs, part]
-            force = drive_recv[pl.ds(step * count + s, 1), :]
-            out = product(later_ref[...], stacked(real, imag))
+        def look(g):
+            part = pl.ds(pl.multiple_of((start + WIDTH * g) * TILE, WIDTH * TILE), WIDTH * TILE)
+            return product(
+                later_ref[...], stacked(dens[0:pairs, part], dens[pairs : 2 * pairs, part])
+            )
+
+        rounds = number // WIDTH
+
+        def one(g, out):
+            after = look(jnp.minimum(g + 1, rounds - 1))
             keep = keep_ref[...]
             spacing = spacing_ref[...]
-            dens[0:pairs, part] = keep * real + spacing * imag + force * out[0:pairs, TILE:]
-            dens[pairs : 2 * pairs, part] = (
-                keep * imag - spacing * real - force * out[0:pairs, 0:TILE]
-            )
-            seen = out[pairs : pairs + 8, 0:TILE] + out[pairs + 8 : pairs + 16, TILE:]
-            coef_next[pl.ds(pl.multiple_of(s * 8, 8), 8), :] = seen + force * shift_rows(seen, 4)
-            return carry
-
-        lax.fori_loop(0, number, one, 0, unroll=4)
+            for w in range(WIDTH):
+                s = start + WIDTH * g + w
+                part = pl.ds(pl.multiple_of(s * TILE, TILE), TILE)
+                left = slice(w * TILE, (w + 1) * TILE)
+                right = slice((WIDTH + w) * TILE, (WIDTH + w + 1) * TILE)
+                real = dens[0:pairs, part]
+                imag = dens[pairs : 2 * pairs, part]
+                force = drive_recv[pl.ds(step * count + s, 1), :]
+                dens[0:pairs, part] = keep * real + spacing * imag + force * out[0:pairs, right]
+                dens[pairs : 2 * pairs, part] = (
+                    keep * imag - spacing * real - force * out[0:pairs, left]
+                )
+                seen = out[pairs : pairs + 8, left] + out[pairs + 8 : pairs + 16, right]
+                coef_next[pl.ds(pl.multiple_of(s * 8, 8), 8), :] = seen + force * shift_rows(
+                    seen, 4
+                )
+            return after
+
+        lax.fori_loop(0, rounds, one, look(0), unroll=UNROLL)
 
     middle = count // 2
 
@@ -568,7 +600,12 @@
 
         @pl.when(step == 0)
         def _():
-            find_places()
+            look_first()
+            send_coef(
+                0,
+                coef_next[pl.ds(4, count, stride=8), :],
+                coef_next[pl.ds(5, count, stride=8), :],
+            )
 
         @pl.when(step >= 1)
         def _():
@@ -609,18 +646,11 @@
 
         return carry
 
+    find_places()
     lax.fori_loop(0, STEPS, one_step, 0)
 
-    for copy in field_stores:
-        copy.start()
     advance(STEPS - 2, middle, count - middle)
     all_drive(STEPS - 1).wait_recv()
-
-    @pl.loop(0, gx)
-    def _(g):
-        advance(STEPS - 1, g * gy, gy)
-        store_group(g).start()
-
     all_dip.wait_send()
 
     @pl.loop(0, STEPS)
@@ -628,6 +658,73 @@
         all_drive(step).wait_send()
         all_coef(step).wait_send()
 
+
+def finish(
+    gx,
+    gy,
+    plane,
+    ep,
+    hp,
+    dens,
+    drive_recv,
+    later_ref,
+    keep_ref,
+    spacing_ref,
+    e_out,
+    h_out,
+    dens_out,
+    fresh,
+    out_sem,
+    field_sem,
+):
+    count = gx * gy
+    cols = e_out.shape[1]
+    pairs = dens.shape[0] // 2
+    group = gy * TILE
+    wide = WIDTH * TILE
+    field_stores = (
+        pltpu.make_async_copy(ep.at[:, 0:cols, :], e_out, field_sem.at[0]),
+        pltpu.make_async_copy(hp.at[:, plane : plane + cols, :], h_out, field_sem.at[1]),
+    )
+    for copy in field_stores:
+        copy.start()
+
+    def store_group(g):
+        part = pl.ds(pl.multiple_of(g * group, group), group)
+        return pltpu.make_async_copy(fresh.at[:, part], dens_out.at[:, part], out_sem.at[g])
+
+    def look(g):
+        part = pl.ds(pl.multiple_of(g * wide, wide), wide)
+        return product(
+            later_ref[0:pairs, :], stacked(dens[0:pairs, part], dens[pairs : 2 * pairs, part])
+        )
+
+    rounds = count // WIDTH
+    per_group = gy // WIDTH
+
+    def one_group(group_at, out):
+        for i in range(per_group):
+            g = group_at * per_group + i
+            after = look(jnp.minimum(g + 1, rounds - 1))
+            keep = keep_ref[...]
+            spacing = spacing_ref[...]
+            for w in range(WIDTH):
+                s = WIDTH * g + w
+                part = pl.ds(pl.multiple_of(s * TILE, TILE), TILE)
+                left = slice(w * TILE, (w + 1) * TILE)
+                right = slice((WIDTH + w) * TILE, (WIDTH + w + 1) * TILE)
+                real = dens[0:pairs, part]
+                imag = dens[pairs : 2 * pairs, part]
+                force = drive_recv[pl.ds((STEPS - 1) * count + s, 1), :]
+                fresh[0:pairs, part] = keep * real + spacing * imag + force * out[:, right]
+                fresh[pairs : 2 * pairs, part] = (
+                    keep * imag - spacing * real - force * out[:, left]
+                )
+            out = after
+        store_group(group_at).start()
+        return out
+
+    lax.fori_loop(0, gx, one_group, look(0))
     for copy in field_stores:
         copy.wait()
 
@@ -656,21 +753,32 @@
     pairs = coupling.shape[0] ** 2
     columns = density.shape[3]
 
+    size = coupling.shape[0]
     vmem = pl.BlockSpec(memory_space=pltpu.VMEM)
-    hbm = pl.BlockSpec(memory_space=pl.ANY)
+    hbm = pl.BlockSpec(memory_space=pltpu.HBM)
     dma = pltpu.SemaphoreType.DMA
     tall = (count, TILE)
-    e_out, h_out, dens_out = pl.pallas_call(
+    padded = jax.ShapeDtypeStruct((3, cols + cy, nz), F32)
+    state = pl.pallas_call(
         functools.partial(kernel, gx, gy, cx, cy),
         out_shape=(
-            jax.ShapeDtypeStruct((3, cols, nz), F32),
-            jax.ShapeDtypeStruct((3, cols, nz), F32),
+            padded,
+            padded,
             jax.ShapeDtypeStruct((2 * pairs, columns), F32),
+            jax.ShapeDtypeStruct((STEPS * count, TILE), F32),
+            jax.ShapeDtypeStruct((pairs + 16, 3 * pairs), BF16),
+            jax.ShapeDtypeStruct((pairs, TILE), F32),
+            jax.ShapeDtypeStruct((pairs, TILE), F32),
         ),
-        in_specs=[vmem] * 6 + [hbm] * 4,
-        out_specs=(hbm, hbm, hbm),
+        in_specs=[hbm] * 10,
+        out_specs=(vmem,) * 7,
         scratch_shapes=[
-            pltpu.VMEM((2 * pairs, columns), F32),
+            pltpu.VMEM((1, size), F32),
+            pltpu.VMEM((size, size), F32),
+            pltpu.VMEM((size, size), F32),
+            pltpu.VMEM((1, count), jnp.int32),
+            pltpu.VMEM((1, count), jnp.int32),
+            pltpu.VMEM((TILE // 2, count), jnp.int32),
             pltpu.VMEM((3, columns), F32),
             pltpu.VMEM((2 * count, 2 * cols), BF16),
             pltpu.VMEM((2 * cols, 2 * count), BF16),
@@ -680,18 +788,12 @@
             pltpu.VMEM((2,) + tall, F32),
             pltpu.VMEM((6,) + tall, F32),
             pltpu.VMEM((16, 3 * pairs), BF16),
-            pltpu.VMEM((pairs + 16, 3 * pairs), BF16),
-            pltpu.VMEM((pairs, TILE), F32),
-            pltpu.VMEM((pairs, TILE), F32),
-            pltpu.VMEM((3, cols + cy, nz), F32),
-            pltpu.VMEM((3, cols + cy, nz), F32),
             pltpu.VMEM((2, cx, nz), F32),
             pltpu.VMEM((2, cx, nz), F32),
             pltpu.VMEM((2, cx, nz), F32),
             pltpu.VMEM((2, cx, nz), F32),
             pltpu.VMEM((4 * count, TILE), F32),
             pltpu.VMEM((4 * count, TILE), F32),
-            pltpu.VMEM((STEPS * count, TILE), F32),
             pltpu.VMEM((STEPS * count, TILE), F32),
             pltpu.VMEM((STEPS * 2 * count, TILE), F32),
             pltpu.VMEM((STEPS * 2 * count, TILE), F32),
@@ -704,24 +806,40 @@
             dma((STEPS,)),
             dma((STEPS,)),
             dma((gx,)),
-            dma((gx,)),
+            dma((6,)),
             dma((3,)),
         ],
         compiler_params=pltpu.CompilerParams(
-            collective_id=0, has_side_effects=True, vmem_limit_bytes=48 * 1024 * 1024
+            collective_id=0, has_side_effects=True, vmem_limit_bytes=24 * 1024 * 1024
         ),
-    )(
+    )(*(pltpu.with_memory_space_constraint(x, pltpu.HBM) for x in (
         levels.reshape(1, -1),
         coupling,
         rates,
         tile_cells.reshape(1, -1),
         tile_owner.reshape(1, -1),
-        emitter_offsets,
+        emitter_offsets.T,
         field_e.reshape(3, cols, nz),
         field_h.reshape(3, cols, nz),
         density.reshape(2 * pairs, columns),
         dipole,
-    )
+    )))
+    e_out, h_out, dens_out = pl.pallas_call(
+        functools.partial(finish, gx, gy, cy),
+        out_shape=(
+            jax.ShapeDtypeStruct((3, cols, nz), F32),
+            jax.ShapeDtypeStruct((3, cols, nz), F32),
+            jax.ShapeDtypeStruct((2 * pairs, columns), F32),
+        ),
+        in_specs=[vmem] * 7,
+        out_specs=(hbm, hbm, hbm),
+        scratch_shapes=[
+            pltpu.VMEM((2 * pairs, columns), F32),
+            dma((gx,)),
+            dma((2,)),
+        ],
+        compiler_params=pltpu.CompilerParams(vmem_limit_bytes=24 * 1024 * 1024),
+    )(*state)
     return (
         e_out.reshape(field_e.shape),
         h_out.reshape(field_h.shape),

time: 152 us -> 80.3 us (0.53)
  Pallas kernels: 134 us -> 79.5 us
  local copies, waits for them, and re-layouts: 16.7 us -> 0 us
    pallas_call x1 -> x2, Pallas kernels: 134 us -> 79.5 us  [the longest x1 73.8 us: body(): pl.pallas_call(functools.partial(kernel, gx, gy, cx, cy), out_shape=(padd...]
    unnamed x20 -> x0, local copies, waits for them, and re-layouts: 16.7 us -> none
where the time goes in v2:
time: 80.3 us; the launch traced here: 80.2 us
  Pallas kernels  79.5 us (99%)
    pallas_call x1, Pallas kernels, body(): pl.pallas_call(functools.partial(kernel, gx, gy, cx, cy), out_shape=(padd...  73.8 us
    pallas_call x1, Pallas kernels, body(): pl.pallas_call(functools.partial(finish, gx, gy, cy), out_shape=(jax.Shap...  5.78 us

profile of v2, /device:TPU:1, one launch (start us, length us, event | category | flops | bytes accessed | tf_op | source)
XLA Modules:
  0.0 80.2 jit_solution(6590487589744188537)
XLA Ops:
  0.6 73.8 %shard_map.121 = (f32[3,272,256]{2,1,0:T(8,128)S(1)}, f32[3,272,256]{2,1,0:T(8,128)S(1)}, f32[128,16384]{1,0:T(8,128)S(1)}, f32[512,128]{1,0:T(8,128)S(1)}, bf16...) custom-call(f32[1,8]{1,0:T(1,128)} %bitcast.14, f32[8,8]{1,0:T(8,128)} %coupling_hbm.1, ...), custom_call_target="tpu_custom_call" | custom-call | tf_op jit(solution)/shard_map/pallas_call | solution.py:762
  74.4 5.8 %shard_map.122 = (f32[3,256,256]{2,1,0:T(8,128)}, f32[3,256,256]{2,1,0:T(8,128)}, f32[128,16384]{1,0:T(8,128)}) custom-call(f32[3,272,256]{2,1,0:T(8,128)S(1)} %get-tuple-element.13.ep, f32[3,272,256]{2,1,0:T(8,128)S(1)} %get-tuple-element.14.hp, f32[128,16384]{1,0:T(8,128)S(1)} %get-tuple-element.15.dens, f32[512,128]{1,0:T(8,128)S(1)} %get-tuple-element.16.drive_recv, ...), custom_call_target="tpu_custom_call" | custom-call | tf_op jit(solution)/shard_map/pallas_call | solution.py:827

commit v3 on v2

--- a/solution.py
+++ b/solution.py
@@ -12,6 +12,7 @@
 COURANT = 0.5
 TIME_STEP = 0.12
 WIDTH = 2
+FIRST = 4
 UNROLL = 4
 
 MESH = pl.DeviceIdType.MESH
@@ -97,7 +98,7 @@
     spacing = TIME_STEP * jnp.sum((first - second) * levels, axis=1, keepdims=True)
 
     sym_row, decay_row, spacing_row = as_row(sym), as_row(decay), as_row(spacing)
-    rows = iota((8, pairs), 0)
+    rows = iota((16, pairs), 0)
 
     def free(real, imag):
         keep = 1.0 - decay_row
@@ -114,22 +115,27 @@
             free_imag + shift_rows(driven_imag, distance),
         )
 
-    push = exact(jnp.broadcast_to(sym_row, (8, pairs)), commute)
+    push = exact(jnp.broadcast_to(sym_row, (16, pairs)), commute)
     real_zero = jnp.where(rows == 0, -sym_row * decay_row, 0.0)
     imag_zero = jnp.where(rows == 0, sym_row * spacing_row, jnp.where(rows == 1, push, 0.0))
     real_one, imag_one = both(real_zero, imag_zero, 2)
     real_two, imag_two = both(real_one, imag_one, 4)
+    real_three, imag_three = both(real_two, imag_two, 8)
 
     def parts(matrix):
         high, low = split(matrix)
         return jnp.concatenate([high, high, low], axis=1)
 
+    def opening(zero, one, two):
+        return one + shift_rows(zero, 4) + shift_rows(two, 8)
+
     begin = parts(
         jnp.concatenate(
-            [real_one + shift_rows(real_zero, 4), imag_one + shift_rows(imag_zero, 4)], axis=0
+            [opening(real_zero, real_one, real_two), opening(imag_zero, imag_one, imag_two)],
+            axis=0,
         )
     )
-    later = parts(jnp.concatenate([commute, real_two, imag_two], axis=0))
+    later = parts(jnp.concatenate([commute, real_three, imag_three], axis=0))
     keep = jnp.broadcast_to(1.0 - decay, (pairs, TILE))
     spacing = jnp.broadcast_to(spacing, (pairs, TILE))
     return begin, later, keep, spacing
@@ -179,9 +185,16 @@
     dip_send,
     dip_recv,
     drive_send,
-    coef_send,
-    coef_recv,
-    coef_next,
+    coef0_send,
+    coef0_recv,
+    coef1_send,
+    coef1_recv,
+    coef2_send,
+    coef2_recv,
+    coef3_send,
+    coef3_recv,
+    looked,
+    ahead,
     halo_send,
     halo_recv,
     dip_sems,
@@ -267,15 +280,32 @@
             device_id_type=MESH,
         )
 
+    drive_sems = [(drive_ssem.at[step], drive_rsem.at[step]) for step in range(STEPS)]
+    coefs = [
+        (send, recv, width, coef_ssem.at[step], coef_rsem.at[step])
+        for step, (send, recv, width) in enumerate(
+            (
+                (coef0_send, coef0_recv, 2),
+                (coef1_send, coef1_recv, 4),
+                (coef2_send, coef2_recv, 4),
+                (coef3_send, coef3_recv, 4),
+            )
+        )
+    ]
+
     def all_drive(step):
-        return whole(
-            drive_send, drive_recv, step * count, 1, drive_ssem.at[step], drive_rsem.at[step]
-        )
+        return whole(drive_send, drive_recv, step * count, 1, *drive_sems[step])
+
+    def send_drive(step):
+        to_all(drive_send, drive_recv, step * count, 1, 1, *drive_sems[step])
 
     def all_coef(step):
-        return whole(
-            coef_send, coef_recv, step * 2 * count, 2, coef_ssem.at[step], coef_rsem.at[step]
-        )
+        send, recv, width, out_sem, back_sem = coefs[step]
+        return whole(send, recv, 0, width, out_sem, back_sem)
+
+    def send_coef(step):
+        send, recv, width, out_sem, back_sem = coefs[step]
+        to_all(send, recv, 0, width, width, out_sem, back_sem)
 
     all_dip = whole(dip_send, dip_recv, 0, 4, dip_sems.at[0], dip_sems.at[1])
 
@@ -357,20 +387,29 @@
         def _(g):
             load_group(g).wait()
 
-        def one(s, carry):
-            part = pl.ds(pl.multiple_of(s * TILE, TILE), TILE)
+        def one(g, carry):
+            part = pl.ds(pl.multiple_of(g * FIRST * TILE, FIRST * TILE), FIRST * TILE)
             state = stacked(dens[0:pairs, part], dens[pairs : 2 * pairs, part])
             seen = product(begin_ref[...], state)
-            coef_next[pl.ds(pl.multiple_of(s * 8, 8), 8), :] = seen[0:8, 0:TILE] + seen[8:16, TILE:]
+            seen = seen[0:16, 0 : FIRST * TILE] + seen[16:32, FIRST * TILE :]
+            for w in range(FIRST):
+                rows = pl.ds(pl.multiple_of((g * FIRST + w) * 16, 16), 16)
+                looked[rows, :] = seen[:, w * TILE : (w + 1) * TILE]
             return carry
 
-        lax.fori_loop(0, count, one, 0, unroll=4)
-
-    def send_coef(step, alpha, beta):
-        base = step * 2 * count
-        coef_send[pl.ds(base, count, stride=2), :] = alpha
-        coef_send[pl.ds(base + 1, count, stride=2), :] = beta
-        to_all(coef_send, coef_recv, base, 2, 2, coef_ssem.at[step], coef_rsem.at[step])
+        lax.fori_loop(0, count // FIRST, one, 0, unroll=4)
+        for k in range(4):
+            coef1_send[pl.ds(k, count, stride=4), :] = looked[pl.ds(k, count, stride=16), :]
+        for k in range(2):
+            coef0_send[pl.ds(k, count, stride=2), :] = looked[pl.ds(4 + k, count, stride=16), :]
+
+    def combine(target, source, first, stride, step):
+        force = drive_recv[step * count : (step + 1) * count, :]
+        for k in range(4):
+            target[pl.ds(k, count, stride=4), :] = (
+                source[pl.ds(first + k, count, stride=stride), :]
+                + force * source[pl.ds(first + k + 4, count, stride=stride), :]
+            )
 
     lane = iota((count, TILE), 1)
     sub = iota((count, TILE), 0)
@@ -543,10 +582,12 @@
                 ep[c, 0:cols, part] = ep[c, 0:cols, part] - change[h * cols : (h + 1) * cols, :]
 
     def advance(step, start, number):
+        height = pairs + 32 if step == 0 else pairs
+
         def look(g):
             part = pl.ds(pl.multiple_of((start + WIDTH * g) * TILE, WIDTH * TILE), WIDTH * TILE)
             return product(
-                later_ref[...], stacked(dens[0:pairs, part], dens[pairs : 2 * pairs, part])
+                later_ref[0:height, :], stacked(dens[0:pairs, part], dens[pairs : 2 * pairs, part])
             )
 
         rounds = number // WIDTH
@@ -567,94 +608,92 @@
                 dens[pairs : 2 * pairs, part] = (
                     keep * imag - spacing * real - force * out[0:pairs, left]
                 )
-                seen = out[pairs : pairs + 8, left] + out[pairs + 8 : pairs + 16, right]
-                coef_next[pl.ds(pl.multiple_of(s * 8, 8), 8), :] = seen + force * shift_rows(
-                    seen, 4
-                )
+                if step == 0:
+                    seen = out[pairs : pairs + 16, left] + out[pairs + 16 : pairs + 32, right]
+                    rows = pl.ds(pl.multiple_of(s * 8, 8), 8)
+                    ahead[rows, :] = seen[0:8, :] + force * seen[8:16, :]
             return after
 
         lax.fori_loop(0, rounds, one, look(0), unroll=UNROLL)
 
-    middle = count // 2
-
-    def one_step(step, carry):
-        @pl.when(step >= 2)
-        def _():
-            advance(step - 2, middle, count - middle)
-
-        @pl.when(step >= 1)
-        def _():
-            all_drive(step - 1).wait_recv()
-            force = drive_recv[pl.ds(pl.multiple_of((step - 1) * count, count), count), :]
-
-            def coef(k):
-                return coef_next[pl.ds(k, count, stride=8), :]
-
-            send_coef(step, coef(0) + force * coef(2), coef(1) + force * coef(3))
-
+    def drive_of(step):
+        return drive_send[step * count : (step + 1) * count, :]
+
+    def moved_at(step):
+        recv, width = coefs[step][1], coefs[step][2]
+        terms = [recv[pl.ds(k, count, stride=width), :] for k in range(width)]
+        back = step - (width.bit_length() - 2)
+        while len(terms) > 1:
+            half = len(terms) // 2
+            force = drive_of(back)
+            terms = [terms[k] + force * terms[k + half] for k in range(half)]
+            back += 1
+        return terms[0]
+
+    def until_h(step):
         e_plane.wait_recv()
         e_row.wait_recv()
         step_h()
         h_row.start()
         h_plane.start()
 
-        @pl.when(step == 0)
-        def _():
-            look_first()
-            send_coef(
-                0,
-                coef_next[pl.ds(4, count, stride=8), :],
-                coef_next[pl.ds(5, count, stride=8), :],
-            )
-
-        @pl.when(step >= 1)
-        def _():
-            advance(step - 1, 0, middle)
-
+    def until_drive(step):
         e_plane.wait_send()
         e_row.wait_send()
         h_plane.wait_recv()
         h_row.wait_recv()
         step_e()
-
-        @pl.when(step == 0)
-        def _():
+        if step == 0:
             all_dip.wait_recv()
-
-        drive = sampled_drive()
-        drive_send[pl.ds(pl.multiple_of(step * count, count), count), :] = drive
-        to_all(
-            drive_send,
-            drive_recv,
-            step * count,
-            1,
-            1,
-            drive_ssem.at[step],
-            drive_rsem.at[step],
-        )
+        drive_send[step * count : (step + 1) * count, :] = sampled_drive()
         h_plane.wait_send()
         h_row.wait_send()
+
+    def until_e(step):
         all_coef(step).wait_recv()
-        base = step * 2 * count
-        alpha = coef_recv[pl.ds(base, count, stride=2), :]
-        beta = coef_recv[pl.ds(base + 1, count, stride=2), :]
-        feed_field(alpha + drive * beta)
-
-        @pl.when(step < STEPS - 1)
-        def _():
+        feed_field(moved_at(step))
+        if step < STEPS - 1:
             send_e()
 
-        return carry
+    half = count // 2
+    quarter = count // 4
 
     find_places()
-    lax.fori_loop(0, STEPS, one_step, 0)
-
-    advance(STEPS - 2, middle, count - middle)
-    all_drive(STEPS - 1).wait_recv()
+    until_h(0)
+    look_first()
+    send_coef(0)
+    until_drive(0)
+    until_e(0)
+    send_drive(0)
+    send_coef(1)
+    until_h(1)
+    all_drive(0).wait_recv()
+    combine(coef2_send, looked, 8, 16, 0)
+    send_coef(2)
+    until_drive(1)
+    until_e(1)
+    send_drive(1)
+    advance(0, 0, half)
+    until_h(2)
+    advance(0, half, half)
+    all_drive(1).wait_recv()
+    combine(coef3_send, ahead, 0, 8, 1)
+    send_coef(3)
+    until_drive(2)
+    until_e(2)
+    send_drive(2)
+    advance(1, 0, half)
+    until_h(3)
+    advance(1, half, half)
+    all_drive(2).wait_recv()
+    advance(2, 0, quarter)
+    until_drive(3)
+    send_drive(3)
+    until_e(3)
+    advance(2, quarter, count - quarter)
+    all_drive(3).wait_recv()
     all_dip.wait_send()
-
-    @pl.loop(0, STEPS)
-    def _(step):
+    for step in range(STEPS):
         all_drive(step).wait_send()
         all_coef(step).wait_send()
 
@@ -766,7 +805,7 @@
             padded,
             jax.ShapeDtypeStruct((2 * pairs, columns), F32),
             jax.ShapeDtypeStruct((STEPS * count, TILE), F32),
-            jax.ShapeDtypeStruct((pairs + 16, 3 * pairs), BF16),
+            jax.ShapeDtypeStruct((pairs + 32, 3 * pairs), BF16),
             jax.ShapeDtypeStruct((pairs, TILE), F32),
             jax.ShapeDtypeStruct((pairs, TILE), F32),
         ),
@@ -787,7 +826,7 @@
             pltpu.VMEM((2,) + tall, jnp.int32),
             pltpu.VMEM((2,) + tall, F32),
             pltpu.VMEM((6,) + tall, F32),
-            pltpu.VMEM((16, 3 * pairs), BF16),
+            pltpu.VMEM((32, 3 * pairs), BF16),
             pltpu.VMEM((2, cx, nz), F32),
             pltpu.VMEM((2, cx, nz), F32),
             pltpu.VMEM((2, cx, nz), F32),
@@ -795,8 +834,15 @@
             pltpu.VMEM((4 * count, TILE), F32),
             pltpu.VMEM((4 * count, TILE), F32),
             pltpu.VMEM((STEPS * count, TILE), F32),
-            pltpu.VMEM((STEPS * 2 * count, TILE), F32),
-            pltpu.VMEM((STEPS * 2 * count, TILE), F32),
+            pltpu.VMEM((2 * count, TILE), F32),
+            pltpu.VMEM((2 * count, TILE), F32),
+            pltpu.VMEM((4 * count, TILE), F32),
+            pltpu.VMEM((4 * count, TILE), F32),
+            pltpu.VMEM((4 * count, TILE), F32),
+            pltpu.VMEM((4 * count, TILE), F32),
+            pltpu.VMEM((4 * count, TILE), F32),
+            pltpu.VMEM((4 * count, TILE), F32),
+            pltpu.VMEM((16 * count, TILE), F32),
             pltpu.VMEM((8 * count, TILE), F32),
             dma((4,)),
             dma((4,)),

time: 80.3 us -> 78.7 us (0.980)
  Pallas kernels: 79.5 us -> 77.9 us
    pallas_call x1, Pallas kernels: 73.8 us -> 72.3 us  [body(): pl.pallas_call(functools.partial(kernel, gx, gy, cx, cy), out_shape=(padd...]
where the time goes in v3:
time: 78.7 us; the launch traced here: 78.6 us
  Pallas kernels  77.9 us (99%)
    pallas_call x1, Pallas kernels, body(): pl.pallas_call(functools.partial(kernel, gx, gy, cx, cy), out_shape=(padd...  72.3 us
    pallas_call x1, Pallas kernels, body(): pl.pallas_call(functools.partial(finish, gx, gy, cy), out_shape=(jax.Shap...  5.64 us

profile of v3, /device:TPU:1, one launch (start us, length us, event | category | flops | bytes accessed | tf_op | source)
XLA Modules:
  0.0 78.6 jit_solution(13169792983199238465)
XLA Ops:
  0.6 72.3 %shard_map.121 = (f32[3,272,256]{2,1,0:T(8,128)S(1)}, f32[3,272,256]{2,1,0:T(8,128)S(1)}, f32[128,16384]{1,0:T(8,128)S(1)}, f32[512,128]{1,0:T(8,128)S(1)}, bf16...) custom-call(f32[1,8]{1,0:T(1,128)} %bitcast.14, f32[8,8]{1,0:T(8,128)} %coupling_hbm.1, ...), custom_call_target="tpu_custom_call" | custom-call | tf_op jit(solution)/shard_map/pallas_call | solution.py:801
  72.9 5.6 %shard_map.122 = (f32[3,256,256]{2,1,0:T(8,128)}, f32[3,256,256]{2,1,0:T(8,128)}, f32[128,16384]{1,0:T(8,128)}) custom-call(f32[3,272,256]{2,1,0:T(8,128)S(1)} %get-tuple-element.13.ep, f32[3,272,256]{2,1,0:T(8,128)S(1)} %get-tuple-element.14.hp, f32[128,16384]{1,0:T(8,128)S(1)} %get-tuple-element.15.dens, f32[512,128]{1,0:T(8,128)S(1)} %get-tuple-element.16.drive_recv, ...), custom_call_target="tpu_custom_call" | custom-call | tf_op jit(solution)/shard_map/pallas_call | solution.py:873

commit v4 on v3

--- a/solution.py
+++ b/solution.py
@@ -378,9 +378,6 @@
     for copy in field_loads:
         copy.wait()
 
-    pl.semaphore_wait(barrier, count - 1)
-    send_e()
-    to_all(dip_send, dip_recv, 0, 4, 4, dip_sems.at[0], dip_sems.at[1])
 
     def look_first():
         @pl.loop(0, gx)
@@ -655,12 +652,16 @@
         if step < STEPS - 1:
             send_e()
 
+    find_places()
+    pl.semaphore_wait(barrier, count - 1)
+    send_e()
+    to_all(dip_send, dip_recv, 0, 4, 4, dip_sems.at[0], dip_sems.at[1])
+
     half = count // 2
     quarter = count // 4
 
-    find_places()
+    look_first()
     until_h(0)
-    look_first()
     send_coef(0)
     until_drive(0)
     until_e(0)

time: 78.7 us -> 76.5 us (0.972); the launches traced: 78.6 us -> 75 us
  Pallas kernels: 77.9 us -> 74.4 us
    pallas_call x1, Pallas kernels: 72.3 us -> 68.7 us  [body(): pl.pallas_call(functools.partial(kernel, gx, gy, cx, cy), out_shape=(padd...]
where the time goes in v4:
time: 76.5 us; the launch traced here: 75 us
  Pallas kernels  74.4 us (97%)
    pallas_call x1, Pallas kernels, body(): pl.pallas_call(functools.partial(kernel, gx, gy, cx, cy), out_shape=(padd...  68.7 us
    pallas_call x1, Pallas kernels, body(): pl.pallas_call(functools.partial(finish, gx, gy, cy), out_shape=(jax.Shap...  5.64 us

profile of v4, /device:TPU:1, one launch (start us, length us, event | category | flops | bytes accessed | tf_op | source)
XLA Modules:
  0.0 75.0 jit_solution(3130413187929433059)
XLA Ops:
  0.6 68.7 %shard_map.121 = (f32[3,272,256]{2,1,0:T(8,128)S(1)}, f32[3,272,256]{2,1,0:T(8,128)S(1)}, f32[128,16384]{1,0:T(8,128)S(1)}, f32[512,128]{1,0:T(8,128)S(1)}, bf16...) custom-call(f32[1,8]{1,0:T(1,128)} %bitcast.14, f32[8,8]{1,0:T(8,128)} %coupling_hbm.1, ...), custom_call_target="tpu_custom_call" | custom-call | tf_op jit(solution)/shard_map/pallas_call | solution.py:802
  69.4 5.6 %shard_map.122 = (f32[3,256,256]{2,1,0:T(8,128)}, f32[3,256,256]{2,1,0:T(8,128)}, f32[128,16384]{1,0:T(8,128)}) custom-call(f32[3,272,256]{2,1,0:T(8,128)S(1)} %get-tuple-element.13.ep, f32[3,272,256]{2,1,0:T(8,128)S(1)} %get-tuple-element.14.hp, f32[128,16384]{1,0:T(8,128)S(1)} %get-tuple-element.15.dens, f32[512,128]{1,0:T(8,128)S(1)} %get-tuple-element.16.drive_recv, ...), custom_call_target="tpu_custom_call" | custom-call | tf_op jit(solution)/shard_map/pallas_call | solution.py:874
